TPU v7x, 1024 devices: a whole 4x4x32 slice. The times are simulated.
1024 devices in a mesh: fsdp: 64 (over x_lo, z), tp: 16 (over x_hi, y, core).
Axes of the slice: x: 4 (x_hi: 2, x_lo: 2; x = x_hi * 2 + x_lo), y: 4, z: 32, core: 2. Of those that a mesh axis runs over, the one named last changes fastest.
Arguments:
- dec_query: bfloat16 [64, 2, 4096], P('fsdp'), may hold values from -200 to 200
- new_keys: bfloat16 [64, 2, 512], P('fsdp'), may hold values from -6 to 6
- new_values: bfloat16 [64, 2, 512], P('fsdp'), may hold values from -6 to 6
- cache_keys: bfloat16 [64, 2048, 512], P('fsdp', 'tp'), may hold values from -6 to 6
- cache_values: bfloat16 [64, 2048, 512], P('fsdp', 'tp'), may hold values from -6 to 6
- lengths: int32 [64], P('fsdp'), may hold values from 256 to 2048, as said below
- out_weight: bfloat16 [4096, 4096], P('fsdp', 'tp'), may hold values from -0.09375 to 0.09375
- train_attn: bfloat16 [8192, 4096], P('fsdp', 'tp'), may hold values from -0.15625 to 0.15625
- grad_out: bfloat16 [8192, 4096], P('fsdp'), may hold values from -16 to 16
Outputs:
- dec_out: bfloat16 [64, 2, 4096], P('fsdp', None, 'tp')
- grad_attn: bfloat16 [8192, 4096], P('fsdp', 'tp')
- grad_weight: float32 [4096, 4096], P('fsdp', 'tp')
Inputs may be any that keep to these rules, and one draw needn't show every extreme that they name: `lengths`: the length 2048 occurs.
All inputs are finite; a program needn't handle non-finite values.
Results may differ from a plain program's by a relative error of at most 0.0049.
Values may be sent and summed in bfloat16 or wider, within the bound.
A program may use at most 32 MiB of HBM per device.

v0:
```python
import jax
import jax.numpy as jnp
from jax import lax
from jax.sharding import PartitionSpec as P

QH = 32
KVH = 4
HD = 128
GROUP = 8


NEG_FILL = -1e30


def combined_all(part, axis, combine):
    gathered = jax.tree.map(lambda a: lax.all_gather(a, axis), part)

    def take(source):
        return jax.tree.map(lambda a: lax.dynamic_index_in_dim(a, source, 0, False), gathered)

    return lax.fori_loop(
        1, lax.axis_size(axis), lambda source, state: combine(state, take(source)), take(0)
    )


def combine_pair(left_part, right_part):
    highest = jnp.maximum(left_part[0], right_part[0])
    scale_left = jnp.exp(left_part[0] - highest)
    scale_right = jnp.exp(right_part[0] - highest)
    totals = left_part[1] * scale_left + right_part[1] * scale_right
    weighted = left_part[2] * scale_left[..., None] + right_part[2] * scale_right[..., None]
    return (highest, totals, weighted)


def shards(
    dec_query,
    new_keys,
    new_values,
    cache_keys,
    cache_values,
    lengths,
    out_weight,
    train_attn,
    grad_out,
):
    row_count, step_count, _ = dec_query.shape
    cache_len = cache_keys.shape[1]
    tp_size = lax.axis_size("tp")
    tp_index = lax.axis_index("tp")
    heads_dev = QH // tp_size
    head_first = tp_index * heads_dev
    scaling = 1.0 / HD**0.5
    weights = lax.all_gather(out_weight, "fsdp", axis=0, tiled=True)
    key_cache = cache_keys.reshape(row_count, cache_len, KVH, HD)
    value_cache = cache_values.reshape(row_count, cache_len, KVH, HD).astype(jnp.float32)
    positions = tp_index * cache_len + jnp.arange(cache_len, dtype=jnp.int32)
    usable = positions[None, :] < lengths[:, None]
    key_heads = jnp.repeat(new_keys.reshape(row_count, step_count, KVH, HD), GROUP, axis=2)
    value_heads = jnp.repeat(new_values.reshape(row_count, step_count, KVH, HD), GROUP, axis=2)
    key_own = lax.dynamic_slice_in_dim(key_heads, head_first, heads_dev, 2)
    value_own = lax.dynamic_slice_in_dim(value_heads, head_first, heads_dev, 2).astype(jnp.float32)

    def cache_partial(queries):
        step_span = queries.shape[1]
        grouped = queries.reshape(row_count, step_span, KVH, GROUP, HD)
        scores = (
            jnp.einsum("rsgqd,rpgd->rsgqp", grouped, key_cache, preferred_element_type=jnp.float32)
            * scaling
        )
        allowed = usable[:, None, None, None, :]
        maxima = jnp.max(jnp.where(allowed, scores, NEG_FILL), axis=-1)
        exp_terms = jnp.where(allowed, jnp.exp(scores - maxima[..., None]), 0.0)
        totals = jnp.sum(exp_terms, axis=-1)
        weighted = jnp.einsum(
            "rsgqp,rpgd->rsgqd", exp_terms, value_cache, precision=lax.Precision.HIGHEST
        )
        return (
            maxima.reshape(row_count, step_span, QH),
            totals.reshape(row_count, step_span, QH),
            weighted.reshape(row_count, step_span, QH, HD),
        )

    def decode_block(queries, step_ids):
        step_span = queries.shape[1]
        maxima, totals, weighted = cache_partial(queries)
        maxima, totals, weighted = combined_all((maxima, totals, weighted), "tp", combine_pair)
        maxima = lax.dynamic_slice_in_dim(maxima, head_first, heads_dev, 2)
        totals = lax.dynamic_slice_in_dim(totals, head_first, heads_dev, 2)
        weighted = lax.dynamic_slice_in_dim(weighted, head_first, heads_dev, 2)
        own_query = lax.dynamic_slice_in_dim(
            queries.reshape(row_count, step_span, QH, HD), head_first, heads_dev, 2
        )
        new_scores = (
            jnp.einsum("rshd,rjhd->rshj", own_query, key_own, preferred_element_type=jnp.float32)
            * scaling
        )
        step_allowed = (
            jnp.arange(step_count, dtype=jnp.int32)[None, :]
            <= jnp.array(step_ids, jnp.int32)[:, None]
        )
        allowed = step_allowed[None, :, None, :]
        new_maxima = jnp.max(jnp.where(allowed, new_scores, NEG_FILL), axis=-1)
        new_terms = jnp.where(allowed, jnp.exp(new_scores - new_maxima[..., None]), 0.0)
        new_totals = jnp.sum(new_terms, axis=-1)
        new_weighted = jnp.einsum(
            "rshj,rjhd->rshd", new_terms, value_own, precision=lax.Precision.HIGHEST
        )
        highest, totals_all, weighted_all = combine_pair(
            (maxima, totals, weighted), (new_maxima, new_totals, new_weighted)
        )
        attended = (
            (weighted_all / totals_all[..., None])
            .astype(jnp.bfloat16)
            .reshape(row_count, step_span, heads_dev * HD)
        )
        partial_out = lax.dot_general(
            attended, weights, (((2,), (1,)), ((), ())), preferred_element_type=jnp.float32
        )
        return lax.psum_scatter(partial_out, "tp", scatter_dimension=2, tiled=True).astype(
            jnp.bfloat16
        )

    decoded = [decode_block(dec_query[:, step : step + 1], [step]) for step in range(step_count)]
    dec_out = jnp.concatenate(decoded, axis=1)
    grad_attn = jnp.dot(grad_out, weights, preferred_element_type=jnp.float32).astype(jnp.bfloat16)
    grad_weight = lax.psum_scatter(
        lax.dot_general(
            grad_out, train_attn, (((0,), (0,)), ((), ())), preferred_element_type=jnp.float32
        ),
        "fsdp",
        scatter_dimension=0,
        tiled=True,
    )
    return (dec_out, grad_attn, grad_weight)


def solution(mesh):
    return jax.shard_map(
        shards,
        mesh=mesh,
        in_specs=(
            P("fsdp", None, None),
            P("fsdp", None, None),
            P("fsdp", None, None),
            P("fsdp", "tp", None),
            P("fsdp", "tp", None),
            P("fsdp"),
            P("fsdp", "tp"),
            P("fsdp", "tp"),
            P("fsdp", None),
        ),
        out_specs=(P("fsdp", None, "tp"), P("fsdp", "tp"), P("fsdp", "tp")),
        check_vma=False,
    )
```

profile of v0, /device:TPU:24, one launch (start us, length us, event | category | flops | bytes accessed | tf_op | source)
XLA Modules:
  0.0 806.3 jit_solution(11280301096941272568)
XLA Ops:
  7.2 0.7 all-gather.2.cloned.1.call-update
  8.0 0.9 slice_reduce_fusion.1
  8.9 0.9 reshape.312
  10.5 0.9 reshape.315
  11.4 0.2 fusion.16
  11.6 0.3 select_reduce_fusion.1
  11.8 0.1 all_gather_reshape.18
  11.9 0.2 bitcast_reduce_fusion.1
  12.1 0.3 convolution_bitcast_fusion.3
  12.4 0.3 convolution_bitcast_fusion.2
  12.7 0.1 all_gather_reshape.21
  12.8 0.1 all_gather_reshape.19
  12.9 27.6 %all_gather.22 = f32[16,1,1,32]{3,2,1,0:T(1,128)S(1)} all-gather(f32[1,1,1,32]{3,2,1,0:T(1,128)S(1)} %all_gather_reshape.19), channel_id=1, replica_groups=mesh['fsdp'=64,'tp'=16] {'tp'}, dimensions={0}, use_global_device_ids=true | all-gather | bytes 2176 | tf_op jit(solution)/shard_map/all_gather | solution.py:16
  40.4 19.7 %all_gather.23 = f32[16,1,1,32,128]{4,3,2,1,0:T(8,128)S(1)} all-gather(f32[1,1,1,32,128]{4,3,2,1,0:T(8,128)S(1)} %convolution_bitcast_fusion.3), channel_id=1, replica_groups=mesh['fsdp'=64,'tp'=16] {'tp'}, dimensions={0}, use_global_device_ids=true | all-gather | bytes 278528 | tf_op jit(solution)/shard_map/all_gather | solution.py:16
  60.1 20.9 %all_gather.21 = f32[16,1,1,32]{3,2,1,0:T(1,128)S(1)} all-gather(f32[1,1,1,32]{3,2,1,0:T(1,128)S(1)} %all_gather_reshape.18), channel_id=1, replica_groups=mesh['fsdp'=64,'tp'=16] {'tp'}, dimensions={0}, use_global_device_ids=true | all-gather | bytes 2176 | tf_op jit(solution)/shard_map/all_gather | solution.py:16
  81.0 1.9 while.38
  81.0 0.1 fusion.93
  81.2 0.1 fusion.93
  81.3 0.1 fusion.93
  81.4 0.1 fusion.93
  82.9 0.1 all_gather_reshape.22
  83.0 19.3 %all_gather.26 = f32[16,1,1,32]{3,2,1,0:T(1,128)S(1)} all-gather(f32[1,1,1,32]{3,2,1,0:T(1,128)S(1)} %all_gather_reshape.22), channel_id=1, replica_groups=mesh['fsdp'=64,'tp'=16] {'tp'}, dimensions={0}, use_global_device_ids=true | all-gather | bytes 2176 | tf_op jit(solution)/shard_map/all_gather | solution.py:16
  102.3 21.3 %all_gather.27 = f32[16,1,1,32,128]{4,3,2,1,0:T(8,128)S(1)} all-gather(f32[1,1,1,32,128]{4,3,2,1,0:T(8,128)S(1)} %convolution_bitcast_fusion.2), channel_id=1, replica_groups=mesh['fsdp'=64,'tp'=16] {'tp'}, dimensions={0}, use_global_device_ids=true | all-gather | bytes 278528 | tf_op jit(solution)/shard_map/all_gather | solution.py:16
  123.6 19.3 %all_gather.25 = f32[16,1,1,32]{3,2,1,0:T(1,128)S(1)} all-gather(f32[1,1,1,32]{3,2,1,0:T(1,128)S(1)} %all_gather_reshape.21), channel_id=1, replica_groups=mesh['fsdp'=64,'tp'=16] {'tp'}, dimensions={0}, use_global_device_ids=true | all-gather | bytes 2176 | tf_op jit(solution)/shard_map/all_gather | solution.py:16
  142.9 1.9 while.39
  144.9 0.1 fusion.42
  145.0 0.1 select_reduce_fusion.3
  145.2 0.2 fusion.72
  145.4 0.1 fusion.69
  145.4 0.1 fusion.46
  145.7 0.1 fusion.40
  145.8 0.1 select_reduce_fusion.2
  145.9 0.2 fusion.73
  146.1 0.1 fusion.67
  146.2 0.1 fusion.44
  146.4 130.0 %all-gather.2.cloned.1.call-done = bf16[4096,256]{1,0:T(8,128)(2,1)} async-done(((bf16[64,256]{1,0:T(8,128)(2,1)}), bf16[4096,256]{1,0:T(8,128)(2,1)}) %all-gather.2.cloned.1.call-update) | async-done | bytes 2097168 | tf_op jit(solution)/shard_map/all_gather | solution.py:53
  276.4 3.6 convolution_bitcast_fusion.1
  280.1 1.5 copy-done.1
  281.6 2.0 convolution_bitcast_fusion
  283.7 0.8 copy-done.2
  284.4 2.7 fusion.74
  287.1 1.1 convolution_convert_fusion
  288.2 101.8 %reduce-scatter.10.cloned.1.call-done = f32[256,1]{1,0:T(8,128)} async-done(((f32[4096,1]{1,0:T(8,128)}), f32[256,1]{1,0:T(8,128)}) %reduce-scatter.10.cloned.1.call-update) | async-done | bytes 1040
  390.0 1.0 copy.37
  391.0 129.2 %reduce-scatter.12.cloned.1.call-done = f32[256,1]{1,0:T(8,128)} async-done(((f32[4096,1]{1,0:T(8,128)}), f32[256,1]{1,0:T(8,128)}) %reduce-scatter.12.cloned.1.call-update) | async-done | bytes 1040
  520.2 1.0 copy.39
  521.2 0.6 pad_maximum_fusion
  521.8 278.0 %reduce-scatter.8.cloned.1.call-done = f32[64,256]{1,0:T(8,128)} async-done(((f32[4096,256]{1,0:T(8,128)}), f32[64,256]{1,0:T(8,128)}) %reduce-scatter.8.cloned.1.call-update) | async-done | bytes 65552 | tf_op jit(solution)/shard_map/reduce_scatter | solution.py:126
  (151 shorter events, 3.7 us)
Async XLA Ops:
  7.2 276.5 %copy-start = (bf16[128,4096]{1,0:T(8,128)(2,1)S(1)}, bf16[128,4096]{1,0:T(8,128)(2,1)}, u32[]{:S(2)}) copy-start(bf16[128,4096]{1,0:T(8,128)(2,1)} %param.23) | copy-start | bytes 3145732
  7.2 137.6 %copy-start.3 = (bf16[1,2,512]{2,1,0:T(2,128)(2,1)S(1)}, bf16[1,2,512]{2,1,0:T(2,128)(2,1)}, u32[]{:S(2)}) copy-start(bf16[1,2,512]{2,1,0:T(2,128)(2,1)} %param.17) | copy-start | bytes 6148
  7.2 137.6 %copy-start.4 = (bf16[1,2,512]{2,1,0:T(2,128)(2,1)S(1)}, bf16[1,2,512]{2,1,0:T(2,128)(2,1)}, u32[]{:S(2)}) copy-start(bf16[1,2,512]{2,1,0:T(2,128)(2,1)} %param.16) | copy-start | bytes 6148
  7.2 269.2 %all-gather.2.cloned.1.call-start = ((), (), s32[]{:S(2)}) async-start(), calls=%async_computation.3 | async-start | bytes 2129920 | tf_op jit(solution)/shard_map/all_gather | solution.py:53
  7.9 382.1 %reduce-scatter.10.cloned.1.call-start = ((), (), s32[]{:S(2)}) async-start(), calls=%async_computation.5 | async-start | bytes 2228224
  280.0 1.6 copy-start.1
  280.0 240.2 %reduce-scatter.12.cloned.1.call-start = ((), (), s32[]{:S(2)}) async-start(), calls=%async_computation.6 | async-start | bytes 2228224
  283.6 0.8 copy-start.2
  283.6 516.2 %reduce-scatter.8.cloned.1.call-start = ((), (), s32[]{:S(2)}) async-start(), calls=%async_computation.4 | async-start | bytes 4259840 | tf_op jit(solution)/shard_map/reduce_scatter | solution.py:126
Sparse Core Ops, SparseCore 0:
  10.7 265.6 all-gather.1
  282.3 107.6 reduce-scatter.9
  395.9 124.2 reduce-scatter.11
  524.0 275.6 reduce-scatter.7
where the time goes:
time: 807 us; the launch traced here: 806 us
  waiting for transfers between devices  640 us (79%)
  blocking collectives  128 us (16%)
  between operations  14.6 us (2%)
  matrix products  10.8 us (1%)
    reduce_scatter x1, waiting for transfers between devices, shards(): lax.psum_scatter(lax.dot_general(grad_out, train_attn, (((0,), (0,)), (()...  278 us
    unnamed x6, waiting for transfers between devices  232 us
    all_gather x1, waiting for transfers between devices, shards(): weights = lax.all_gather(out_weight, 'fsdp', axis=0, tiled=True)  130 us
    all_gather x6, blocking collectives, combined_all(): gathered = jax.tree.map(lambda a: lax.all_gather(a, axis), part)  128 us
  transfers between devices with their start and end apart: 4, of which 4 were waited for; matrix products, arithmetic and copies ran while one was open for 2% of the time, Pallas kernels for 0%

commit v1 on v0

v1 whole, which is shorter than its diff:
```python
import functools

import jax
import jax.numpy as jnp
from jax import lax
from jax.experimental import pallas as pl
from jax.experimental.pallas import tpu as pltpu
from jax.sharding import PartitionSpec as P

HD = 128
NEG_FILL = -1e30
MESH = pl.DeviceIdType.MESH
F32 = jnp.float32
BF16 = jnp.bfloat16
NEAR = BF16
NARROW_HOPS = 4


def kernel(
    fs, tp,
    q_hbm, nk_hbm, nv_hbm, ck_hbm, cv_hbm, len_ref, w_hbm, ta_hbm, g_hbm,
    dec_ref, ga_ref, gw_ref,
    q_ref, nk_ref, nv_ref, ck_ref, cv_ref, ta2, g_ref, in_s,
    wfull, part, gacc, gin, nbs, nbr, snd16, rcv16, snd32, rcv32, qs, att, sa, ra, sb, rb,
    ag_s, ag_r, fw_s, fw_r, ax_s, ax_r, nb_s, nb_r, rs_s, rs_r, g_s, g_r, t_s, t_r, a_s, a_r, b_s, b_r,
):
    ring = fs // 2
    half = ring // 2
    hops = half // 2
    rows = w_hbm.shape[0]
    cols = w_hbm.shape[1]
    tokens = ta_hbm.shape[0]
    hcols = cols // 2
    steps = q_ref.shape[1]
    heads = q_ref.shape[2] // HD
    kv_heads = nk_ref.shape[2] // HD
    group = heads // kv_heads
    heads_dev = heads // tp
    unit = heads_dev * steps
    dout = fs * rows
    dcols = dout // tp
    span = ring * rows

    f = lax.axis_index("fsdp")
    t = lax.axis_index("tp")
    xl = f // ring
    z = f % ring
    zp = (xl * ring + (z + 1) % ring, t)
    zm = (xl * ring + (z + ring - 1) % ring, t)
    zp2 = (xl * ring + (z + 2) % ring, t)
    zm2 = (xl * ring + (z + ring - 2) % ring, t)
    xp = ((f + ring) % fs, t)
    gp = ((f + ring) % fs, (t + tp // 2) % tp)

    def peer(k):
        return (t + k) % tp

    own_rows = pl.ds(pl.multiple_of(f * rows, rows), rows)
    loads = [
        pltpu.make_async_copy(a, b, in_s.at[i])
        for i, (a, b) in enumerate((
            (w_hbm, wfull.at[own_rows, :]), (ta_hbm, ta2.at[0:tokens, :]), (g_hbm, g_ref), (q_hbm, q_ref),
            (nk_hbm, nk_ref), (nv_hbm, nv_ref), (ck_hbm, ck_ref), (cv_hbm, cv_ref),
        ))
    ]
    barrier = pltpu.get_barrier_semaphore()
    for dev in (zp, zm, zp2, zm2, xp, gp):
        pl.semaphore_signal(barrier, inc=1, device_id=dev, device_id_type=MESH)

    def greet(k, _):
        pl.semaphore_signal(barrier, inc=1, device_id=(f, peer(k)), device_id_type=MESH)
        return 0

    lax.fori_loop(1, tp, greet, 0)
    for load in loads:
        load.start()

    def remote(src, dst, s_sem, r_sem, dev):
        return pltpu.make_async_remote_copy(
            src_ref=src, dst_ref=dst, send_sem=s_sem, recv_sem=r_sem,
            device_id=dev, device_id_type=MESH,
        )

    def shard(owner):
        return wfull.at[pl.ds(pl.multiple_of((xl * ring + owner) * rows, rows), rows), :]

    def even_owner(d, s):
        return (z + ring - 2 * s) % ring if d == 0 else (z + 2 * s) % ring

    def odd_owner(d, k):
        return (z + ring - 2 * k - 1) % ring if d == 0 else (z + 2 * k + 1) % ring

    def ag(d, s, first=False):
        place = shard(even_owner(d, s - 1))
        return remote(w_hbm if first else place, place, ag_s.at[d, s - 1], ag_r.at[d, s - 1],
                      zp2 if d == 0 else zm2)

    def fw(d, k, first=False):
        place = shard(even_owner(d, k))
        return remote(w_hbm if first else place, place, fw_s.at[d, k], fw_r.at[d, k],
                      zp if d == 0 else zm)

    def ax(owner, first=False):
        place = shard(owner)
        k = (owner + ring - z) % ring
        return remote(w_hbm if first else place, place, ax_s.at[k], ax_r.at[k], xp)

    def block(owner, h):
        return part.at[pl.ds(pl.multiple_of(owner * rows, rows), rows), h * hcols:(h + 1) * hcols]

    def ahead(d, distance):
        return (z + distance) % ring if d == 0 else (z + ring - distance) % ring

    def nb(d, k):
        return remote(nbs.at[d, k], nbr.at[d, k], nb_s.at[d, k], nb_r.at[d, k],
                      zp if d == 0 else zm)

    def send_nb(d, k):
        for h in range(2):
            nbs[d, k, :, h * hcols:(h + 1) * hcols] = (
                block(ahead(d, 2 * k + 1), h)[...].astype(NEAR)
            )
        nb(d, k).start()

    def bufs(s):
        return (snd16, rcv16) if s <= NARROW_HOPS else (snd32, rcv32)

    def rs(d, h, s):
        src, dst = bufs(s)
        return remote(src.at[d, h, s - 1], dst.at[d, h, s - 1], rs_s.at[d, h, s - 1],
                      rs_r.at[d, h, s - 1], zp2 if d == 0 else zm2)

    def rs_step(d, s):
        k = hops - s + 1 - d
        if k < hops:
            nb(d, k).wait_recv()
        for h in range(2):
            total = block(ahead(d, 2 * k), h)[...]
            if k < hops:
                total += nbr[d, k, :, h * hcols:(h + 1) * hcols].astype(F32)
            if s > 1:
                rs(d, h, s - 1).wait_recv()
                total += bufs(s - 1)[1][d, h, s - 2].astype(F32)
            src = bufs(s)[0]
            src[d, h, s - 1] = total.astype(src.dtype)
            rs(d, h, s).start()

    def pair_of(i):
        off = ((i + 1) // 2) * (1 - 2 * ((i + 1) % 2))
        return ((z + half) // 2 + off + ring) % half

    def gx(i):
        at = pl.multiple_of((1 - xl) * span + pair_of(i) * (2 * rows), 2 * rows)
        return remote(g_hbm.at[:, pl.ds(at, 2 * rows)], gin.at[i], g_s.at[i], g_r.at[i], gp)

    tax = remote(ta_hbm, ta2.at[tokens:2 * tokens, :], t_s, t_r, xp)

    def axa(k):
        return remote(sa.at[peer(k)], ra.at[t], a_s.at[k - 1], a_r.at[k - 1], (f, peer(k)))

    def axb(k):
        return remote(sb.at[peer(k)], rb.at[t], b_s.at[k - 1], b_r.at[k - 1], (f, peer(k)))

    def tdot(a, b):
        return lax.dot_general(a, b, (((0,), (0,)), ((), ())), preferred_element_type=F32)

    def ndot(a, b):
        return lax.dot_general(a, b, (((1,), (1,)), ((), ())), preferred_element_type=F32)

    pl.semaphore_wait(barrier, 6 + tp - 1)

    ag(0, 1, True).start()
    ag(1, 1, True).start()
    fw(0, 0, True).start()
    fw(1, 0, True).start()
    tax.start()
    gx(0).start()
    gx(1).start()
    gx(2).start()
    gx(3).start()
    ax(z, True).start()

    def send_g(i, _):
        gx(i).start()
        return 0

    lax.fori_loop(4, half, send_g, 0)

    for i in (3, 4, 5, 6, 7):
        loads[i].wait()

    qf = q_ref[0].astype(F32)
    for h in range(heads):
        qs[h * steps:(h + 1) * steps, :] = qf[:, h * HD:(h + 1) * HD]
    scaling = 1.0 / HD**0.5
    length = len_ref[0]
    span_q = group * steps
    npos = ck_ref.shape[1]
    pos = t * npos + lax.broadcasted_iota(jnp.int32, (span_q, npos), 1)
    ok = pos < length
    step_of = lax.broadcasted_iota(jnp.int32, (span_q, 1), 0) % steps
    for g in range(kv_heads):
        lanes = slice(g * HD, (g + 1) * HD)
        q32 = qs[g * span_q:(g + 1) * span_q, :]
        sc = ndot(q32.astype(BF16), ck_ref[0, :, lanes]) * scaling
        sc = jnp.where(ok, sc, NEG_FILL)
        new = []
        top = jnp.max(sc, axis=-1, keepdims=True)
        for j in range(steps):
            key = nk_ref[0, j:j + 1, lanes].astype(F32)
            sj = jnp.sum(q32 * key, axis=-1, keepdims=True) * scaling
            oj = jnp.logical_and(step_of >= j, t == 0)
            sj = jnp.where(oj, sj, NEG_FILL)
            new.append((sj, oj))
            top = jnp.maximum(top, sj)
        pr = jnp.where(ok, jnp.exp(sc - top), 0.0)
        hi = pr.astype(BF16)
        lo = (pr - hi.astype(F32)).astype(BF16)
        val = cv_ref[0, :, lanes]
        wt = jnp.dot(hi, val, preferred_element_type=F32) + jnp.dot(
            lo, val, preferred_element_type=F32
        )
        tot = jnp.sum(pr, axis=-1, keepdims=True)
        for j in range(steps):
            sj, oj = new[j]
            pj = jnp.where(oj, jnp.exp(sj - top), 0.0)
            tot = tot + pj
            wt = wt + pj * nv_ref[0, j:j + 1, lanes].astype(F32)
        topb = jnp.broadcast_to(top, (span_q, HD))
        totb = jnp.broadcast_to(tot, (span_q, HD))
        for j in range(group // heads_dev):
            dest = g * (group // heads_dev) + j
            mine = slice(j * unit, (j + 1) * unit)
            sa[dest, 0:unit, :] = wt[mine]
            sa[dest, unit:2 * unit, :] = topb[mine]
            sa[dest, 2 * unit:3 * unit, :] = totb[mine]
    ra[t] = sa[t]

    def send_a(k, _):
        axa(k).start()
        return 0

    lax.fori_loop(1, tp, send_a, 0)

    def ag_step(s, mode):
        for d in range(2 if mode > 0 else 1):
            ag(d, s).wait_recv()
            if mode == 2 or (mode == 1 and d == 0):
                ag(d, s + 1).start()
            if mode > 0:
                fw(d, s).start()
            ax(even_owner(d, s)).start()
        for d in range(2):
            fw(d, s - 1).wait_recv()
            ax(odd_owner(d, s - 1)).start()

    def g_step(i):
        gx(i).wait_recv()
        pair = pair_of(i)
        at = pl.multiple_of(xl * span + pair * (2 * rows), 2 * rows)
        both = jnp.concatenate([g_ref[:, pl.ds(at, 2 * rows)], gin[i]], axis=0)
        here = pl.ds(pl.multiple_of(pair * (2 * rows), 2 * rows), 2 * rows)
        part[here, :] = tdot(both, ta2[...])

    per_dest = dcols // (2 * rows)

    def use_pair(n):
        off = ((n + 1) // 2) * (1 - 2 * ((n + 1) % 2))
        pair = (z // 2 + off + half) % half
        for e in range(2):
            ax((2 * pair + e) % ring).wait_recv()
        places, gs, ws = [], [], []
        for c in (xl, 1 - xl):
            place = c * half + pair
            at = pl.ds(pl.multiple_of(place * (2 * rows), 2 * rows), 2 * rows)
            places.append(place)
            gs.append(g_ref[:, at])
            ws.append(wfull[at, :])
        wide = jnp.concatenate(ws, axis=0)
        gacc[...] += jnp.dot(
            jnp.concatenate(gs, axis=1), wide, preferred_element_type=F32
        )
        out = ndot(att[...].astype(BF16), wide)[0:8]
        for e, place in enumerate(places):
            lane = pl.ds(pl.multiple_of((place % per_dest) * (2 * rows), 2 * rows), 2 * rows)
            sb[place // per_dest, :, lane] = out[:, e * 2 * rows:(e + 1) * 2 * rows]

    for i in (0, 1, 2):
        loads[i].wait()
    ag_step(1, min(hops - 1, 2))
    tax.wait_recv()
    for i in range(4):
        g_step(i)
    for d in range(2):
        send_nb(d, hops - 1)
    gacc[...] = jnp.zeros_like(gacc)

    def combine():
        def wait_a(k, _):
            axa(k).wait_recv()
            return 0

        lax.fori_loop(1, tp, wait_a, 0)
        tops = ra[:, unit:2 * unit, :]
        scale = jnp.exp(tops - jnp.max(tops, axis=0, keepdims=True))
        total = jnp.sum(ra[:, 2 * unit:3 * unit, :] * scale, axis=0)
        mixed = jnp.sum(ra[:, 0:unit, :] * scale, axis=0) / total
        att[...] = jnp.zeros_like(att)
        for hh in range(heads_dev):
            att[0:steps, hh * HD:(hh + 1) * HD] = mixed[hh * steps:(hh + 1) * steps]

    def send_b(k, _):
        axb(k).start()
        return 0

    used = 0
    for s in range(1, hops + 1):
        rs_step(0, s)
        if s < hops:
            rs_step(1, s)
        if s < hops:
            ag_step(s + 1, min(hops - s - 1, 2))
        for i in (2 * s + 2, 2 * s + 3):
            if i < half:
                g_step(i)
        if s < hops:
            for d in range(2):
                send_nb(d, hops - 1 - s)
        if s == 3:
            combine()
        if s > 3:
            more = min(3, 2 * s - 2 - used)
            lax.fori_loop(used, used + more, lambda n, c: (use_pair(n), c)[1], 0)
            used += more
    if hops <= 3:
        combine()
    lax.fori_loop(used, half, lambda n, c: (use_pair(n), c)[1], 0)
    lax.fori_loop(1, tp, send_b, 0)
    rb[t] = sb[t]
    ga_ref[...] = gacc[...].astype(BF16)

    for d in range(2):
        nb(d, 0).wait_recv()
    for h in range(2):
        at = slice(h * hcols, (h + 1) * hcols)
        total = block(z, h)[...] + nbr[0, 0, :, at].astype(F32) + nbr[1, 0, :, at].astype(F32)
        for d in range(2):
            rs(d, h, hops - d).wait_recv()
            total += bufs(hops - d)[1][d, h, hops - d - 1].astype(F32)
        gw_ref[:, at] = total

    def wait_b(k, _):
        axb(k).wait_recv()
        return 0

    lax.fori_loop(1, tp, wait_b, 0)
    dec_ref[0] = jnp.sum(rb[...], axis=0)[0:steps].astype(BF16)

    tax.wait_send()

    def drain_tp(k, _):
        axa(k).wait_send()
        axb(k).wait_send()
        return 0

    lax.fori_loop(1, tp, drain_tp, 0)

    def drain_g(i, _):
        gx(i).wait_send()
        return 0

    lax.fori_loop(0, half, drain_g, 0)

    def drain_x(k, _):
        ax((z + k) % ring).wait_send()
        return 0

    lax.fori_loop(0, ring, drain_x, 0)
    for d in range(2):
        def drain_z(s, _, d=d):
            ag(d, s).wait_send()
            return 0

        lax.fori_loop(1, hops + 1 - d, drain_z, 0)

        def drain_f(k, _, d=d):
            fw(d, k).wait_send()
            return 0

        lax.fori_loop(0, hops, drain_f, 0)
        def drain_n(k, _, d=d):
            nb(d, k).wait_send()
            return 0

        lax.fori_loop(0, hops, drain_n, 0)
        for h in range(2):
            for s in range(1, hops + 1 - d):
                rs(d, h, s).wait_send()


def solution(mesh):
    fs, tp = mesh.shape["fsdp"], mesh.shape["tp"]
    ring = fs // 2
    half = ring // 2
    hops = half // 2

    def shards(q, nk, nv, ck, cv, lengths, w, ta, g):
        rows, cols = w.shape
        tokens = ta.shape[0]
        heads = q.shape[2] // HD
        steps = q.shape[1]
        dcols = fs * rows // tp
        dma = pltpu.SemaphoreType.DMA
        vmem = pl.BlockSpec(memory_space=pltpu.VMEM)
        hbm = pl.BlockSpec(memory_space=pltpu.HBM)
        smem = pl.BlockSpec(memory_space=pltpu.SMEM)
        return pl.pallas_call(
            functools.partial(kernel, fs, tp),
            out_shape=(
                jax.ShapeDtypeStruct((1, steps, dcols), BF16),
                jax.ShapeDtypeStruct((tokens, cols), BF16),
                jax.ShapeDtypeStruct((rows, cols), F32),
            ),
            in_specs=[hbm] * 5 + [smem] + [hbm] * 3,
            out_specs=(vmem,) * 3,
            scratch_shapes=[
                pltpu.VMEM(q.shape, BF16), pltpu.VMEM(nk.shape, BF16), pltpu.VMEM(nv.shape, BF16),
                pltpu.VMEM(ck.shape, BF16), pltpu.VMEM(cv.shape, BF16),
                pltpu.VMEM((2 * tokens, cols), BF16), pltpu.VMEM(g.shape, BF16), dma((8,)),
                pltpu.VMEM((fs * rows, cols), BF16),
                pltpu.VMEM((ring * rows, cols), F32),
                pltpu.VMEM((tokens, cols), F32),
                pltpu.VMEM((half, tokens, 2 * rows), BF16),
                pltpu.VMEM((2, hops, rows, cols), NEAR), pltpu.VMEM((2, hops, rows, cols), NEAR),
                pltpu.VMEM((2, 2, hops, rows, cols // 2), BF16),
                pltpu.VMEM((2, 2, hops, rows, cols // 2), BF16),
                pltpu.VMEM((2, 2, hops, rows, cols // 2), F32),
                pltpu.VMEM((2, 2, hops, rows, cols // 2), F32),
                pltpu.VMEM((heads * steps, HD), F32),
                pltpu.VMEM((16, cols), F32),
                pltpu.VMEM((tp, 16, HD), F32),
                pltpu.VMEM((tp, 16, HD), F32),
                pltpu.VMEM((tp, 8, dcols), F32),
                pltpu.VMEM((tp, 8, dcols), F32),
                dma((2, hops)), dma((2, hops)),
                dma((2, hops)), dma((2, hops)),
                dma((ring,)), dma((ring,)),
                dma((2, hops)), dma((2, hops)),
                dma((2, 2, hops)), dma((2, 2, hops)),
                dma((half,)), dma((half,)),
                dma, dma,
                dma((tp - 1,)), dma((tp - 1,)),
                dma((tp - 1,)), dma((tp - 1,)),
            ],
            compiler_params=pltpu.CompilerParams(
                collective_id=0, has_side_effects=True, vmem_limit_bytes=48 * 1024 * 1024
            ),
        )(*[pltpu.with_memory_space_constraint(a, pltpu.HBM) for a in (q, nk, nv, ck, cv)],
          lengths, *[pltpu.with_memory_space_constraint(a, pltpu.HBM) for a in (w, ta, g)])

    return jax.shard_map(
        shards,
        mesh=mesh,
        in_specs=(
            P("fsdp", None, None), P("fsdp", None, None), P("fsdp", None, None),
            P("fsdp", "tp", None), P("fsdp", "tp", None), P("fsdp"),
            P("fsdp", "tp"), P("fsdp", "tp"), P("fsdp", None),
        ),
        out_specs=(P("fsdp", None, "tp"), P("fsdp", "tp"), P("fsdp", "tp")),
        check_vma=False,
    )
```

time: 807 us -> 83.8 us (0.10)
  the two profiles are of different devices: /device:TPU:24 before, /device:TPU:1 now
where the time goes in v1:
time: 83.8 us; the launch traced here: 83.6 us
  Pallas kernels  80.5 us (96%)
  local copies, waits for them, and re-layouts  1.82 us (2%)
  between operations  1.29 us (2%)
    pallas_call x1, Pallas kernels, shards(): pl.pallas_call(functools.partial(kernel, fs, tp), out_shape=(jax.ShapeDty...  80.5 us
    unnamed x3, local copies, waits for them, and re-layouts  1.82 us

profile of v1, /device:TPU:1, one launch (start us, length us, event | category | flops | bytes accessed | tf_op | source)
XLA Modules:
  0.0 83.6 jit_solution(2846192935787077053)
XLA Ops:
  1.3 80.5 %shard_map.112 = (bf16[1,2,256]{2,1,0:T(2,128)(2,1)S(1)}, bf16[128,256]{1,0:T(8,128)(2,1)S(1)}, f32[64,256]{1,0:T(8,128)S(1)}) custom-call(bf16[1,2,4096]{2,1,0:T(2,128)(2,1)} %q_hbm.1, bf16[1,2,512]{2,1,0:T(2,128)(2,1)} %nk_hbm.1, bf16[1,2,512]{2,1,0:T(2,128)(2,1)} %nv_hbm.1, bf16[1,128,512]{2,1,0:T(8,128)(2,1)} %ck_hbm.1, bf16[1,128,512]{2,1,0:T(8,128)(2,1)} %cv_hbm.1, ...), custom_call_target="tpu_custom_call" | custom-call | tf_op jit(solution)/shard_map/pallas_call | solution.py:417
  81.8 0.6 copy.16
  82.3 0.6 copy.17
  83.0 0.6 copy.18

commit v2 on v1

--- a/solution.py
+++ b/solution.py
@@ -315,11 +315,15 @@
 
     used = 0
     for s in range(1, hops + 1):
-        rs_step(0, s)
-        if s < hops:
+        if s == 1:
+            rs_step(0, s)
             rs_step(1, s)
         if s < hops:
             ag_step(s + 1, min(hops - s - 1, 2))
+        if s > 1:
+            rs_step(0, s)
+            if s < hops:
+                rs_step(1, s)
         for i in (2 * s + 2, 2 * s + 3):
             if i < half:
                 g_step(i)

time: 83.8 us -> 80.6 us (0.962)
  Pallas kernels: 80.5 us -> 77.3 us
    pallas_call x1, Pallas kernels: 80.5 us -> 77.3 us  [shards(): pl.pallas_call(functools.partial(kernel, fs, tp), out_shape=(jax.ShapeDty...]
where the time goes in v2:
time: 80.6 us; the launch traced here: 80.4 us
  Pallas kernels  77.3 us (96%)
  local copies, waits for them, and re-layouts  1.82 us (2%)
  between operations  1.29 us (2%)
    pallas_call x1, Pallas kernels, shards(): pl.pallas_call(functools.partial(kernel, fs, tp), out_shape=(jax.ShapeDty...  77.3 us
    unnamed x3, local copies, waits for them, and re-layouts  1.82 us

profile of v2, /device:TPU:1, one launch (start us, length us, event | category | flops | bytes accessed | tf_op | source)
XLA Modules:
  0.0 80.4 jit_solution(5246124567922426029)
XLA Ops:
  1.3 77.3 %shard_map.112 = (bf16[1,2,256]{2,1,0:T(2,128)(2,1)S(1)}, bf16[128,256]{1,0:T(8,128)(2,1)S(1)}, f32[64,256]{1,0:T(8,128)S(1)}) custom-call(bf16[1,2,4096]{2,1,0:T(2,128)(2,1)} %q_hbm.1, bf16[1,2,512]{2,1,0:T(2,128)(2,1)} %nk_hbm.1, bf16[1,2,512]{2,1,0:T(2,128)(2,1)} %nv_hbm.1, bf16[1,128,512]{2,1,0:T(8,128)(2,1)} %ck_hbm.1, bf16[1,128,512]{2,1,0:T(8,128)(2,1)} %cv_hbm.1, ...), custom_call_target="tpu_custom_call" | custom-call | tf_op jit(solution)/shard_map/pallas_call | solution.py:421
  78.6 0.6 copy.16
  79.2 0.6 copy.17
  79.8 0.6 copy.18
